TPU v7x, 32 devices: a whole 2x2x4 slice. The times are simulated.
32 devices in a mesh: groups: 2 (over x), tok: 16 (over z, y, core).
Axes of the slice: x: 2, y: 2, z: 4, core: 2. Of those that a mesh axis runs over, the one named last changes fastest.
Arguments:
- tokens: bfloat16 [4096, 3072], P(('groups', 'tok')), parts along dimension 0, may hold values from -6 to 6
- routes: int32 [4096, 2], P(('groups', 'tok')), parts along dimension 0, may hold values from 0 to 7, all different within a row; in each aligned block of 128 rows (0 to 127, 128 to 255, ...) at most 40 rows name the same one
- weights: bfloat16 [32768, 3072], P(('groups', 'tok')), parts along dimension 0, may hold values from -0.109375 to 0.109375
Outputs:
- whitened: bfloat16 [32768, 3072], P(('groups', 'tok')), parts along dimension 0
There are 2 independent parts, one for each index of `groups`. A program takes and returns all parts, laid end to end along the dimension named above; each array names one. Nothing has to cross between parts.
Inputs may be any that keep to these rules, and one draw needn't show every extreme that they name: `routes`: each token names 2 different experts. Within the tokens of one device no expert is named more than 40 times, and in every draw some expert is named exactly 40 times by the tokens of some device.
All inputs are finite; a program needn't handle non-finite values.
Results may differ from a plain program's by a relative error of at most 0.0064.
The roundings to bfloat16 on the way count: a program that leaves them out, or rounds other values in their place, can miss the bound.
Values may be sent and summed in bfloat16 or wider, within the bound.
A program may use at most 256 MiB of HBM per device.

v0:
```python
import jax
import jax.numpy as jnp
from jax import lax
from jax.sharding import PartitionSpec as P

E = 8
NB = 4


damping = 256.0


def partner_2(block, axis, bit):
    count = lax.axis_size(axis)
    route = []
    for low in range(count):
        high = low | 1 << bit
        if high != low and high < count:
            route += [(low, high), (high, low)]
    return lax.ppermute(block, axis, route)


def row_swap(values, bit_pos):
    return partner_2(values, "tok", bit_pos)


def collect_rows(own_piece, slices):
    bit_count = slices.bit_length() - 1
    for bit_pos in range(bit_count):
        partner = row_swap(own_piece, bit_pos)
        own_piece = jnp.concatenate([own_piece, partner], 0)
    return own_piece


def slot_rows(target, slot_total, tokens):
    tok_rows = tokens.shape[0]
    slot_table = (target[None, :] == jnp.arange(slot_total, dtype=jnp.int32)[:, None]).astype(
        jnp.int32
    )
    slot_table = jnp.sum(slot_table.reshape(slot_total, tok_rows, 2), axis=2).astype(jnp.bfloat16)
    return jnp.dot(slot_table, tokens, preferred_element_type=jnp.float32).astype(jnp.bfloat16)


def whole_factor(gathered, band_width):
    bands = [gathered[:, band * band_width : (band + 1) * band_width] for band in range(NB)]
    eye_block = damping * jnp.eye(band_width, dtype=jnp.float32)
    lower = [[None] * NB for _ in range(NB)]
    for section in range(NB):
        column_parts = []
        for later in range(section, NB):
            part = lax.dot_general(
                bands[later],
                bands[section],
                (((0,), (0,)), ((), ())),
                preferred_element_type=jnp.float32,
            )
            for before in range(section):
                part = part - lax.dot_general(
                    lower[later][before],
                    lower[section][before],
                    (((1,), (1,)), ((), ())),
                    preferred_element_type=jnp.float32,
                )
            column_parts.append(part)
        diag_factor = jnp.linalg.cholesky(column_parts[0] + eye_block)
        lower[section][section] = diag_factor.astype(jnp.bfloat16)
        for later in range(section + 1, NB):
            solved = lax.linalg.triangular_solve(
                diag_factor,
                column_parts[later - section],
                left_side=False,
                lower=True,
                transpose_a=True,
            )
            lower[later][section] = solved.astype(jnp.bfloat16)
    return lower


def local(tokens, routes, weights):
    tok_devices = lax.axis_size("tok")
    slices = tok_devices // E
    tok_rows = tokens.shape[0]
    features = tokens.shape[1]
    most_rows = tok_rows * 5 // 16
    picked = routes.reshape(-1)
    onehot = (picked[:, None] == jnp.arange(E, dtype=jnp.int32)[None, :]).astype(jnp.int32)
    before = jnp.cumsum(onehot, axis=0) - onehot
    ranked = jnp.sum(before * onehot, axis=1)
    slot_cap = most_rows // slices
    target = (picked * slices + ranked % slices) * slot_cap + ranked // slices
    packed = slot_rows(target, tok_devices * slot_cap, tokens)
    received = lax.all_to_all(packed, "tok", split_axis=0, concat_axis=0, tiled=True)
    gathered = collect_rows(received, slices)
    band_width = features // NB
    lower = whole_factor(gathered, band_width)
    weight_bands = [weights[:, band * band_width : (band + 1) * band_width] for band in range(NB)]
    outputs = []
    for section in range(NB):
        total = jnp.dot(
            weight_bands[section], lower[section][section], preferred_element_type=jnp.float32
        )
        for later in range(section + 1, NB):
            total = total + jnp.dot(
                weight_bands[later], lower[later][section], preferred_element_type=jnp.float32
            )
        outputs.append(total.astype(jnp.bfloat16))
    return jnp.concatenate(outputs, 1)


def solution(mesh):
    return jax.shard_map(
        local,
        mesh=mesh,
        in_specs=(
            P(("groups", "tok"), None),
            P(("groups", "tok"), None),
            P(("groups", "tok"), None),
        ),
        out_specs=P(("groups", "tok"), None),
        check_vma=False,
    )
```

profile of v0, /device:TPU:29, one launch (start us, length us, event | category | flops | bytes accessed | tf_op | source)
XLA Modules:
  0.0 1087.4 jit_solution(11546805684851722873)
XLA Ops:
  7.5 58.4 %all_to_all.12 = bf16[16,20,3072]{2,1,0:T(8,128)(2,1)} all-to-all(bf16[16,20,3072]{2,1,0:T(8,128)(2,1)S(1)} %all_to_all.8), channel_id=1, replica_groups=mesh['groups'=2,'tok'=16] {'tok'}, dimensions={0} | all-to-all | bytes 3932160 | tf_op jit(solution)/shard_map/all_to_all | solution.py:92
  113.2 11.7 %cholesky.748 = f32[128,128]{1,0:T(8,128)S(1)} custom-call(f32[128,128]{1,0:T(8,128)S(1)} %cholesky.1169), custom_call_target="Cholesky" | custom-call | tf_op jit(solution)/shard_map/jit(cholesky)/cholesky | solution.py:65
  137.0 11.7 %cholesky.769 = f32[128,128]{1,0:T(8,128)S(1)} custom-call(f32[128,128]{1,0:T(8,128)S(1)} %cholesky.1174), custom_call_target="Cholesky" | custom-call | tf_op jit(solution)/shard_map/jit(cholesky)/cholesky | solution.py:65
  161.1 11.9 %cholesky.788 = f32[128,128]{1,0:T(8,128)S(1)} custom-call(f32[128,128]{1,0:T(8,128)S(1)} %cholesky.1179), custom_call_target="Cholesky" | custom-call | tf_op jit(solution)/shard_map/jit(cholesky)/cholesky | solution.py:65
  185.4 11.7 %cholesky.807 = f32[128,128]{1,0:T(8,128)S(1)} custom-call(f32[128,128]{1,0:T(8,128)S(1)} %cholesky.1184), custom_call_target="Cholesky" | custom-call | tf_op jit(solution)/shard_map/jit(cholesky)/cholesky | solution.py:65
  209.1 12.1 %cholesky.824 = f32[128,128]{1,0:T(8,128)S(1)} custom-call(f32[128,128]{1,0:T(8,128)S(1)} %slice_subtract_fusion.79), custom_call_target="Cholesky" | custom-call | tf_op jit(solution)/shard_map/jit(cholesky)/cholesky | solution.py:65
  228.0 17.9 %while.12 = (s32[]{:T(128)}, f32[768,768]{1,0:T(8,128)}, s32[6,2]{0,1:T(2,128)S(1)}, f32[6,128,128]{2,1,0:T(8,128)S(1)}, s32[]{:T(128)}) while((s32[]{:T(128)}, f32[768,768]{1,0:T(8,128)}, s32[6,2]{0,1:T(2,128)S(1)}, f32[6,128,128]{2,1,0:T(8,128)S(1)}, s32[]{:T(128)}) %tuple.158), condition=%wide.while_cond, body=%wide.while_body.sunk | while | flops 2 | bytes 131181 | solution.py:68
  246.0 59.0 %custom-call.60 = f32[6,128,128]{1,2,0:T(8,128)S(1)} custom-call(f32[6,128,128]{2,1,0:T(8,128)S(1)} %get-tuple-element.45), custom_call_target="InvertDiagBlocksLowerTriangular" | custom-call | tf_op jit(solution)/shard_map/triangular_solve/custom-call.5 | solution.py:68
  380.7 11.7 %cholesky.858 = f32[128,128]{1,0:T(8,128)S(1)} custom-call(f32[128,128]{1,0:T(8,128)S(1)} %cholesky.1192), custom_call_target="Cholesky" | custom-call | tf_op jit(solution)/shard_map/jit(cholesky)/cholesky | solution.py:65
  405.7 11.7 %cholesky.879 = f32[128,128]{1,0:T(8,128)S(1)} custom-call(f32[128,128]{1,0:T(8,128)S(1)} %cholesky.1197), custom_call_target="Cholesky" | custom-call | tf_op jit(solution)/shard_map/jit(cholesky)/cholesky | solution.py:65
  429.8 12.1 %cholesky.898 = f32[128,128]{1,0:T(8,128)S(1)} custom-call(f32[128,128]{1,0:T(8,128)S(1)} %cholesky.1202), custom_call_target="Cholesky" | custom-call | tf_op jit(solution)/shard_map/jit(cholesky)/cholesky | solution.py:65
  454.2 11.7 %cholesky.917 = f32[128,128]{1,0:T(8,128)S(1)} custom-call(f32[128,128]{1,0:T(8,128)S(1)} %cholesky.1207), custom_call_target="Cholesky" | custom-call | tf_op jit(solution)/shard_map/jit(cholesky)/cholesky | solution.py:65
  477.9 11.7 %cholesky.934 = f32[128,128]{1,0:T(8,128)S(1)} custom-call(f32[128,128]{1,0:T(8,128)S(1)} %slice_subtract_fusion.78), custom_call_target="Cholesky" | custom-call | tf_op jit(solution)/shard_map/jit(cholesky)/cholesky | solution.py:65
  502.7 17.9 %while.13 = (s32[]{:T(128)}, f32[768,768]{1,0:T(8,128)}, s32[6,2]{0,1:T(2,128)S(1)}, f32[6,128,128]{2,1,0:T(8,128)S(1)}, s32[]{:T(128)}) while((s32[]{:T(128)}, f32[768,768]{1,0:T(8,128)}, s32[6,2]{0,1:T(2,128)S(1)}, f32[6,128,128]{2,1,0:T(8,128)S(1)}, s32[]{:T(128)}) %tuple.167), condition=%wide.while_cond.clone.2, body=%wide.while_body.clone.2.sunk | while | flops 2 | bytes 131181 | solution.py:68
  520.6 59.1 %custom-call.68 = f32[6,128,128]{1,2,0:T(8,128)S(1)} custom-call(f32[6,128,128]{2,1,0:T(8,128)S(1)} %get-tuple-element.48), custom_call_target="InvertDiagBlocksLowerTriangular" | custom-call | tf_op jit(solution)/shard_map/triangular_solve/custom-call.5 | solution.py:68
  665.1 11.7 %cholesky.989 = f32[128,128]{1,0:T(8,128)S(1)} custom-call(f32[128,128]{1,0:T(8,128)S(1)} %cholesky.1220), custom_call_target="Cholesky" | custom-call | tf_op jit(solution)/shard_map/jit(cholesky)/cholesky | solution.py:65
  689.2 11.9 %cholesky.1008 = f32[128,128]{1,0:T(8,128)S(1)} custom-call(f32[128,128]{1,0:T(8,128)S(1)} %cholesky.1225), custom_call_target="Cholesky" | custom-call | tf_op jit(solution)/shard_map/jit(cholesky)/cholesky | solution.py:65
  713.4 11.7 %cholesky.1027 = f32[128,128]{1,0:T(8,128)S(1)} custom-call(f32[128,128]{1,0:T(8,128)S(1)} %cholesky.1230), custom_call_target="Cholesky" | custom-call | tf_op jit(solution)/shard_map/jit(cholesky)/cholesky | solution.py:65
  737.1 12.1 %cholesky.1044 = f32[128,128]{1,0:T(8,128)S(1)} custom-call(f32[128,128]{1,0:T(8,128)S(1)} %slice_subtract_fusion.77), custom_call_target="Cholesky" | custom-call | tf_op jit(solution)/shard_map/jit(cholesky)/cholesky | solution.py:65
  810.6 16.6 %while.14 = (s32[]{:T(128)}, f32[768,768]{1,0:T(8,128)}, s32[6,2]{0,1:T(2,128)S(1)}, f32[6,128,128]{2,1,0:T(8,128)S(1)}, s32[]{:T(128)}) while((s32[]{:T(128)}, f32[768,768]{1,0:T(8,128)}, s32[6,2]{0,1:T(2,128)S(1)}, f32[6,128,128]{2,1,0:T(8,128)S(1)}, s32[]{:T(128)}) %tuple.168), condition=%wide.while_cond.clone.4, body=%wide.while_body.clone.4.sunk | while | flops 2 | bytes 131181 | solution.py:68
  827.2 59.1 %custom-call.75 = f32[6,128,128]{1,2,0:T(8,128)S(1)} custom-call(f32[6,128,128]{2,1,0:T(8,128)S(1)} %get-tuple-element.50), custom_call_target="InvertDiagBlocksLowerTriangular" | custom-call | tf_op jit(solution)/shard_map/triangular_solve/custom-call.5 | solution.py:68
  947.2 11.7 %cholesky.1078 = f32[128,128]{1,0:T(8,128)S(1)} custom-call(f32[128,128]{1,0:T(8,128)S(1)} %cholesky.1238), custom_call_target="Cholesky" | custom-call | tf_op jit(solution)/shard_map/jit(cholesky)/cholesky | solution.py:65
  996.4 11.9 %cholesky.1118 = f32[128,128]{1,0:T(8,128)S(1)} custom-call(f32[128,128]{1,0:T(8,128)S(1)} %cholesky.1248), custom_call_target="Cholesky" | custom-call | tf_op jit(solution)/shard_map/jit(cholesky)/cholesky | solution.py:65
  1044.4 12.0 %cholesky.1154 = f32[128,128]{1,0:T(8,128)S(1)} custom-call(f32[128,128]{1,0:T(8,128)S(1)} %slice_subtract_fusion.76), custom_call_target="Cholesky" | custom-call | tf_op jit(solution)/shard_map/jit(cholesky)/cholesky | solution.py:65
  (395 shorter events, 633.5 us)
Async XLA Ops:
  0.0 3.1 copy-start
  68.4 4.2 collective-permute-start
  74.3 6.3 copy-start.2
  304.9 4.7 copy-start.18
  304.9 5.2 copy-start.5
  313.5 10.0 slice-start
  316.1 7.3 slice-start.1
  323.5 21.7 %copy-start.24 = (bf16[768,768]{0,1:T(8,128)(2,1)}, bf16[768,768]{0,1:T(8,128)(2,1)S(1)}, u32[]{:S(2)}) copy-start(bf16[768,768]{0,1:T(8,128)(2,1)S(1)} %convolution_dynamic-update-slice_fusion.5) | copy-start | bytes 3538948
  342.1 3.1 copy-start.26
  493.9 6.3 copy-start.13
  498.6 3.0 copy-start.3
  598.4 4.9 copy-start.29
  774.1 5.0 copy-start.25
  779.1 28.8 %copy-start.19 = (bf16[768,768]{0,1:T(8,128)(2,1)}, bf16[768,768]{0,1:T(8,128)(2,1)S(1)}, u32[]{:S(2)}) copy-start(bf16[768,768]{0,1:T(8,128)(2,1)S(1)} %convolution_dynamic-update-slice_fusion.3) | copy-start | bytes 3538948
  797.8 5.0 copy-start.30
  802.8 2.6 copy-start.21
  910.3 4.1 copy-start.14
  910.3 4.1 copy-start.15
  1067.0 3.0 copy-start.11
  1067.0 3.3 copy-start.12
  1067.1 3.6 copy-start.20
  1070.6 4.1 copy-start.6
  1070.6 4.2 copy-start.22
  1078.3 8.7 copy-start.1
  (11 other events, 17.5 us)
where the time goes:
time: 1100 us; the launch traced here: 1090 us
  other arithmetic  691 us (63%)
  matrix products  226 us (21%)
  local copies, waits for them, and re-layouts  90.4 us (8%)
  blocking collectives  58.4 us (5%)
  between operations  17 us (2%)
    another operation x91, other arithmetic, whole_factor(): diag_factor = jnp.linalg.cholesky(column_parts[0] + eye_block)  496 us
    another operation x7, other arithmetic, whole_factor(): lax.linalg.triangular_solve(diag_factor, column_parts[later - section], l...  182 us
    another operation x66, matrix products, whole_factor(): lax.linalg.triangular_solve(diag_factor, column_parts[later - section], l...  101 us
    all_to_all x1, blocking collectives, local(): lax.all_to_all(packed, 'tok', split_axis=0, concat_axis=0, tiled=True)  58.4 us
    another operation x58, local copies, waits for them, and re-layouts, whole_factor(): lax.linalg.triangular_solve(diag_factor, column_parts[later - section], l...  52.2 us
    another operation x40, matrix products, whole_factor(): diag_factor = jnp.linalg.cholesky(column_parts[0] + eye_block)  40.2 us
    dot_general x6, matrix products, local(): jnp.dot(weight_bands[later], lower[later][section], preferred_element_typ...  25.6 us
    dot_general x10, matrix products, whole_factor(): lax.dot_general(bands[later], bands[section], (((0,), (0,)), ((), ())), p...  23.1 us
  transfers between devices with their start and end apart: 1, of which 1 were waited for; matrix products, arithmetic and copies ran while one was open for 0% of the time, Pallas kernels for 0%

commit v1 on v0

v1 whole, which is shorter than its diff:
```python
import functools

import jax
import jax.numpy as jnp
from jax import lax
from jax.experimental import pallas as pl
from jax.experimental.pallas import tpu as pltpu
from jax.sharding import PartitionSpec as P

E = 8
NB = 4
BLK = 128
TILE = 256

damping = 256.0


def partner_2(block, axis, bit):
    count = lax.axis_size(axis)
    route = []
    for low in range(count):
        high = low | 1 << bit
        if high != low and high < count:
            route += [(low, high), (high, low)]
    return lax.ppermute(block, axis, route)


def collect_rows(own_piece, slices):
    bit_count = slices.bit_length() - 1
    for bit_pos in range(bit_count):
        partner = partner_2(own_piece, "tok", bit_pos)
        own_piece = jnp.concatenate([own_piece, partner], 0)
    return own_piece


def slot_rows(target, slot_total, tokens):
    tok_rows = tokens.shape[0]
    slot_table = (target[None, :] == jnp.arange(slot_total, dtype=jnp.int32)[:, None]).astype(
        jnp.int32
    )
    slot_table = jnp.sum(slot_table.reshape(slot_total, tok_rows, 2), axis=2).astype(jnp.bfloat16)
    return jnp.dot(slot_table, tokens, preferred_element_type=jnp.float32).astype(jnp.bfloat16)


def spread(row):
    return jnp.broadcast_to(row, (8, BLK))


def inverse_factor(block_ref, inv_ref, beside):
    lane = lax.broadcasted_iota(jnp.int32, (8, BLK), 1)
    sub = lax.broadcasted_iota(jnp.int32, (8, BLK), 0)
    groups = BLK // 8
    rows = [block_ref[8 * r : 8 * r + 8, :] for r in range(groups)]
    for g in range(groups):
        first = 8 * g
        inside = (lane >= first) & (lane < first + 8)
        cols = {
            r: [spread(rows[r][:, first + j : first + j + 1]) for j in range(8)]
            for r in range(g, groups)
        }
        own = jnp.where(inside, jnp.where(lane == first + sub, 1.0, 0.0), rows[g])
        diag = list(cols[g])
        done = jnp.zeros((8, BLK), jnp.float32)
        for j in range(8):
            root = lax.rsqrt(spread(diag[j][j : j + 1, :]))
            recip = root * root
            pivot = spread(own[j : j + 1, :])
            at = sub == j
            done = jnp.where(at, pivot * root, done)
            scaled = pivot * recip
            own = jnp.where(at, scaled, own - diag[j] * scaled)
            for m in range(j + 1, 8):
                step = spread(diag[m][j : j + 1, :]) * recip
                diag[m] = jnp.where(at, step, diag[m] - diag[j] * step)
        inv_ref[first : first + 8, :] = jnp.where(lane <= first + sub, done, 0.0)
        parts = [spread(own[j : j + 1, :]) for j in range(8)]
        for r in range(g + 1, groups):
            total = jnp.where(inside, 0.0, rows[r])
            for j in range(8):
                total = total - cols[r][j] * parts[j]
            rows[r] = total
        beside(g, groups)


def split(value):
    high = value.astype(jnp.bfloat16)
    return high, (value - high.astype(jnp.float32)).astype(jnp.bfloat16)


def solve_tile(left, panel_tile, first_row, first_col):
    high, low = split(panel_tile)
    right = jnp.concatenate([high, low, high], 0)
    value = jnp.dot(left, right, preferred_element_type=jnp.float32)
    row = first_row + lax.broadcasted_iota(jnp.int32, value.shape, 0)
    col = first_col + lax.broadcasted_iota(jnp.int32, value.shape, 1)
    return jnp.where(col >= row, value, 0.0).astype(jnp.bfloat16)


def factor_kernel(x_ref, u_ref, x_t, u_t, wide, held, panel, own_t, left_ref, inv_ref, block_ref):
    features = x_ref.shape[1]
    tiles = features // TILE
    width = features // NB
    panels = width // BLK
    panel[...] = jnp.zeros_like(panel)
    left_ref[...] = jnp.zeros_like(left_ref)

    def band(k, carry):
        low = pl.multiple_of(k * width, width)

        def clear(p, c):
            held[pl.ds(pl.multiple_of(p * BLK, BLK), BLK), :] = jnp.zeros(
                (BLK, features), jnp.bfloat16
            )
            return c

        lax.fori_loop(0, panels + 1, clear, 0)

        def turn(p, c):
            at = pl.multiple_of(p * BLK, BLK)
            x_t[pl.ds(at, BLK), :] = x_ref[:, pl.ds(low + at, BLK)].T

            def turn_u(q, d):
                q_at = pl.multiple_of(q * width, width)
                u_t[pl.ds(at, BLK), pl.ds(q_at, width)] = u_ref[
                    pl.ds(q_at, width), pl.ds(low + at, BLK)
                ].T
                return d

            return lax.fori_loop(0, k, turn_u, c)

        lax.fori_loop(0, panels, turn, 0)

        def deep(t, c):
            at = pl.multiple_of(t * TILE, TILE)
            wide[:, pl.ds(at, TILE)] = jnp.dot(
                x_t[...], x_ref[:, pl.ds(at, TILE)], preferred_element_type=jnp.float32
            )

            def less(q, d):
                q_at = pl.multiple_of(q * width, width)
                wide[:, pl.ds(at, TILE)] -= jnp.dot(
                    u_t[:, pl.ds(q_at, width)],
                    u_ref[pl.ds(q_at, width), pl.ds(at, TILE)],
                    preferred_element_type=jnp.float32,
                )
                return d

            return lax.fori_loop(0, k, less, c)

        lax.fori_loop(k * (width // TILE), tiles, deep, 0)

        def step(p, c):
            r_at = pl.multiple_of(p * BLK, BLK)
            start = pl.multiple_of(low + r_at, BLK)
            left = left_ref[...]
            held[pl.ds(r_at, BLK), pl.ds(start, BLK)] = solve_tile(
                left, panel[:, pl.ds(start, BLK)], start - BLK, start
            )
            own_t[...] = held[0:width, pl.ds(start, BLK)].T
            ident = lax.broadcasted_iota(jnp.int32, (BLK, BLK), 0) == lax.broadcasted_iota(
                jnp.int32, (BLK, BLK), 1
            )
            block_ref[...] = (
                wide[pl.ds(r_at, BLK), pl.ds(start, BLK)]
                + jnp.where(ident, damping, 0.0)
                - jnp.dot(
                    own_t[...],
                    held[0:width, pl.ds(start, BLK)],
                    preferred_element_type=jnp.float32,
                )
            )

            def beside(g, groups):
                for t in range(tiles):
                    if t * groups // tiles == g:
                        cols = slice(t * TILE, (t + 1) * TILE)
                        held[pl.ds(r_at, BLK), cols] = solve_tile(
                            left, panel[:, cols], start - BLK, t * TILE
                        )
                        row = start + lax.broadcasted_iota(jnp.int32, (BLK, TILE), 0)
                        col = t * TILE + lax.broadcasted_iota(jnp.int32, (BLK, TILE), 1)
                        panel[:, cols] = (
                            wide[pl.ds(r_at, BLK), cols]
                            + jnp.where(row == col, damping, 0.0)
                            - jnp.dot(
                                own_t[...],
                                held[0:width, cols],
                                preferred_element_type=jnp.float32,
                            )
                        )

            inverse_factor(block_ref, inv_ref, beside)
            high, rest = split(inv_ref[...])
            left_ref[...] = jnp.concatenate([high, high, rest], 1)
            return c

        lax.fori_loop(0, panels, step, 0)
        left = left_ref[...]

        def last(t, c):
            at = pl.multiple_of(t * TILE, TILE)
            held[width : width + BLK, pl.ds(at, TILE)] = solve_tile(
                left, panel[:, pl.ds(at, TILE)], low + width - BLK, at
            )
            return c

        lax.fori_loop(0, tiles, last, 0)
        left_ref[...] = jnp.zeros_like(left_ref)

        def keep(p, c):
            at = pl.multiple_of(p * BLK, BLK)
            u_ref[pl.ds(low + at, BLK), :] = held[pl.ds(at + BLK, BLK), :]
            return c

        lax.fori_loop(0, panels, keep, 0)
        return carry

    lax.fori_loop(0, NB, band, 0)


def upper_factor(gathered):
    rows, features = gathered.shape
    width = features // NB
    return pl.pallas_call(
        factor_kernel,
        out_shape=jax.ShapeDtypeStruct((features, features), jnp.bfloat16),
        in_specs=[pl.BlockSpec(memory_space=pltpu.VMEM)],
        out_specs=pl.BlockSpec(memory_space=pltpu.VMEM),
        scratch_shapes=[
            pltpu.VMEM((width, rows), jnp.bfloat16),
            pltpu.VMEM((width, features - width), jnp.bfloat16),
            pltpu.VMEM((width, features), jnp.float32),
            pltpu.VMEM((width + BLK, features), jnp.bfloat16),
            pltpu.VMEM((BLK, features), jnp.float32),
            pltpu.VMEM((BLK, width), jnp.bfloat16),
            pltpu.VMEM((BLK, 3 * BLK), jnp.bfloat16),
            pltpu.VMEM((BLK, BLK), jnp.float32),
            pltpu.VMEM((BLK, BLK), jnp.float32),
        ],
        compiler_params=pltpu.CompilerParams(vmem_limit_bytes=63 << 20),
    )(gathered)


def local(tokens, routes, weights):
    tok_devices = lax.axis_size("tok")
    slices = tok_devices // E
    tok_rows = tokens.shape[0]
    features = tokens.shape[1]
    most_rows = tok_rows * 5 // 16
    picked = routes.reshape(-1)
    onehot = (picked[:, None] == jnp.arange(E, dtype=jnp.int32)[None, :]).astype(jnp.int32)
    before = jnp.cumsum(onehot, axis=0) - onehot
    ranked = jnp.sum(before * onehot, axis=1)
    slot_cap = most_rows // slices
    target = (picked * slices + ranked % slices) * slot_cap + ranked // slices
    packed = slot_rows(target, tok_devices * slot_cap, tokens)
    received = lax.all_to_all(packed, "tok", split_axis=0, concat_axis=0, tiled=True)
    gathered = collect_rows(received, slices)
    upper = upper_factor(gathered)
    band_width = features // NB
    outputs = []
    for section in range(NB):
        lo = section * band_width
        outputs.append(
            lax.dot_general(
                weights[:, lo:],
                upper[lo : lo + band_width, lo:],
                (((1,), (1,)), ((), ())),
                preferred_element_type=jnp.float32,
            ).astype(jnp.bfloat16)
        )
    return jnp.concatenate(outputs, 1)


def solution(mesh):
    return jax.shard_map(
        local,
        mesh=mesh,
        in_specs=(
            P(("groups", "tok"), None),
            P(("groups", "tok"), None),
            P(("groups", "tok"), None),
        ),
        out_specs=P(("groups", "tok"), None),
        check_vma=False,
    )
```

time: 1100 us -> 298 us (0.27)
  other arithmetic: 691 us -> 7.2 us
  matrix products: 226 us -> 25 us
  Pallas kernels: 0 us -> 185 us
  local copies, waits for them, and re-layouts: 90.4 us -> 15.2 us
  between operations: 17 us -> 0.1 us
    another operation x100 -> x2, other arithmetic: 679 us -> 0.62 us  [the longest x91 496 us: whole_factor(): diag_factor = jnp.linalg.cholesky(column_parts[0] + eye_block)]
    pallas_call x0 -> x1, Pallas kernels: none -> 185 us  [upper_factor(): pl.pallas_call(factor_kernel, out_shape=jax.ShapeDtypeStruct((features, f...]
    another operation x106 -> x0, matrix products: 142 us -> none  [the longest x66 101 us: whole_factor(): lax.linalg.triangular_solve(diag_factor, column_parts[later - section], l...]
    dot_general x30 -> x4, matrix products: 82.7 us -> 23.1 us  [local(): lax.dot_general(weights[:, lo:], upper[lo:lo + band_width, lo:], (((1,),...]
    another operation x84 -> x1, local copies, waits for them, and re-layouts: 53.1 us -> 0.01 us  [the longest x58 52.2 us: whole_factor(): lax.linalg.triangular_solve(diag_factor, column_parts[later - section], l...]
    unnamed x70 -> x5, local copies, waits for them, and re-layouts: 13 us -> 0.87 us
where the time goes in v1:
time: 298 us; the launch traced here: 295 us
  Pallas kernels  185 us (62%)
  blocking collectives  58.4 us (20%)
  matrix products  25 us (8%)
  local copies, waits for them, and re-layouts  15.2 us (5%)
  other arithmetic  7.2 us (2%)
  waiting for transfers between devices  3.86 us (1%)
    pallas_call x1, Pallas kernels, upper_factor(): pl.pallas_call(factor_kernel, out_shape=jax.ShapeDtypeStruct((features, f...  185 us
    all_to_all x1, blocking collectives, local(): lax.all_to_all(packed, 'tok', split_axis=0, concat_axis=0, tiled=True)  58.4 us
    dot_general x4, matrix products, local(): lax.dot_general(weights[:, lo:], upper[lo:lo + band_width, lo:], (((1,),...  23.1 us
    concatenate x1, local copies, waits for them, and re-layouts, local(): return jnp.concatenate(outputs, 1)  8.61 us
  transfers between devices with their start and end apart: 1, of which 1 were waited for; matrix products, arithmetic and copies ran while one was open for 0% of the time, Pallas kernels for 0%

profile of v1, /device:TPU:29, one launch (start us, length us, event | category | flops | bytes accessed | tf_op | source)
XLA Modules:
  0.0 294.6 jit_solution(7123110232455328444)
XLA Ops:
  0.0 0.9 copy.21
  0.9 0.1 eq.45
  1.0 0.1 eq.41
  1.2 0.6 reduce-window.6
  1.7 0.2 slice_reduce_fusion
  2.0 0.1 fusion.41
  2.1 0.1 reduce_sum.21
  2.2 0.1 copy.23
  2.3 0.7 fusion.44
  3.1 1.9 convolution_convert_fusion
  5.0 2.5 all_to_all.8
  7.5 58.4 %all_to_all.12 = bf16[16,20,3072]{2,1,0:T(8,128)(2,1)} all-to-all(bf16[16,20,3072]{2,1,0:T(8,128)(2,1)S(1)} %all_to_all.8), channel_id=1, replica_groups=mesh['groups'=2,'tok'=16] {'tok'}, dimensions={0} | all-to-all | bytes 3932160 | tf_op jit(solution)/shard_map/all_to_all | solution.py:257
  65.9 2.6 all_to_all.10
  68.4 0.2 collective-permute-start
  68.6 3.9 %collective-permute-done = bf16[320,3072]{1,0:T(8,128)(2,1)S(1)} collective-permute-done((bf16[320,3072]{1,0:T(8,128)(2,1)S(1)}, bf16[320,3072]{1,0:T(8,128)(2,1)S(1)}, u32[]{:S(2)}, u32[]{:S(2)}) %collective-permute-start) | collective-permute-done | bytes 1966112 | tf_op jit(solution)/shard_map/ppermute | solution.py:25
  72.5 2.3 pad_maximum_fusion.1.x_ref
  74.8 184.7 %shard_map.37 = bf16[3072,3072]{1,0:T(8,128)(2,1)} custom-call(bf16[640,3072]{1,0:T(8,128)(2,1)} %pad_maximum_fusion.1.x_ref), custom_call_target="tpu_custom_call" | custom-call | tf_op jit(solution)/shard_map/pallas_call | solution.py:224
  259.5 3.3 %fusion.30 = bf16[1024,768]{0,1:T(8,128)(2,1)S(1)} fusion(bf16[1024,3072]{1,0:T(8,128)(2,1)} %param.5, bf16[3072,3072]{1,0:T(8,128)(2,1)} %shard_map.37), kind=kOutput, calls=%fused_computation.18 | convolution fusion | flops 1208745984 | bytes 4325376 | tf_op jit(solution)/shard_map/dot_general | solution.py:265
  262.8 6.0 %fusion.33 = bf16[1024,768]{0,1:T(8,128)(2,1)S(1)} fusion(bf16[1024,3072]{1,0:T(8,128)(2,1)} %param.5, bf16[3072,3072]{1,0:T(8,128)(2,1)} %shard_map.37), kind=kOutput, calls=%fused_computation.19 | convolution fusion | flops 2416705536 | bytes 7077888 | tf_op jit(solution)/shard_map/dot_general | solution.py:265
  268.8 0.0 copy-done.1
  268.8 6.2 %fusion.25 = bf16[1024,768]{0,1:T(8,128)(2,1)S(1)} fusion(bf16[1024,3072]{1,0:T(8,128)(2,1)} %param.5, bf16[3072,3072]{1,0:T(8,128)(2,1)S(1)} %copy-done.1), kind=kOutput, calls=%fused_computation.17 | convolution fusion | flops 3624665088 | bytes 9830400 | tf_op jit(solution)/shard_map/dot_general | solution.py:265
  275.0 7.6 %fusion.22 = bf16[1024,768]{0,1:T(8,128)(2,1)S(1)} fusion(bf16[1024,3072]{1,0:T(8,128)(2,1)} %param.5, bf16[3072,3072]{1,0:T(8,128)(2,1)S(1)} %copy-done.1), kind=kOutput, calls=%fused_computation.16 | convolution fusion | flops 4832624640 | bytes 12582912 | tf_op jit(solution)/shard_map/dot_general | solution.py:265
  282.6 3.4 %pad_maximum_fusion = bf16[1024,3072]{0,1:T(8,128)(2,1)} fusion(bf16[1024,768]{0,1:T(8,128)(2,1)S(1)} %fusion.30, bf16[1024,768]{0,1:T(8,128)(2,1)S(1)} %fusion.33, bf16[1024,768]{0,1:T(8,128)(2,1)S(1)} %fusion.25, bf16[1024,768]{0,1:T(8,128)(2,1)S(1)} %fusion.22), kind=kLoop, calls=%fused_computation | loop fusion | flops 25165824 | bytes 12582912 | tf_op jit(solution)/shard_map/concatenate | solution.py:272
  286.0 8.6 %copy.27 = bf16[1024,3072]{1,0:T(8,128)(2,1)} copy(bf16[1024,3072]{0,1:T(8,128)(2,1)} %pad_maximum_fusion) | data formatting | bytes 12582912 | tf_op jit(solution)/shard_map/concatenate | solution.py:272
  (7 shorter events, 0.1 us)
Async XLA Ops:
  0.0 3.1 %copy-start = (bf16[128,3072]{1,0:T(8,128)(2,1)S(1)}, bf16[128,3072]{1,0:T(8,128)(2,1)}, u32[]{:S(2)}) copy-start(bf16[128,3072]{1,0:T(8,128)(2,1)} %param.3) | copy-start | bytes 2359300
  68.4 4.0 %collective-permute-start = (bf16[320,3072]{1,0:T(8,128)(2,1)S(1)}, bf16[320,3072]{1,0:T(8,128)(2,1)S(1)}, u32[]{:S(2)}, u32[]{:S(2)}) collective-permute-start(bf16[320,3072]{1,0:T(8,128)(2,1)S(1)} %all_to_all.10), channel_id=1, source_target_pairs={{0,1},{1,0},{2,3},{3,2},{4,5},{5,4},{6,7},{7,6},{8,9},{9,8},{10,11... | collective-permute-start | bytes 5898248 | tf_op jit(solution)/shard_map/ppermute | solution.py:25
  259.5 9.3 %copy-start.1 = (bf16[3072,3072]{1,0:T(8,128)(2,1)S(1)}, bf16[3072,3072]{1,0:T(8,128)(2,1)}, u32[]{:S(2)}) copy-start(bf16[3072,3072]{1,0:T(8,128)(2,1)} %shard_map.37) | copy-start | bytes 56623108

commit v2 on v1

--- a/solution.py
+++ b/solution.py
@@ -15,22 +15,75 @@
 damping = 256.0
 
 
-def partner_2(block, axis, bit):
-    count = lax.axis_size(axis)
-    route = []
-    for low in range(count):
-        high = low | 1 << bit
-        if high != low and high < count:
-            route += [(low, high), (high, low)]
-    return lax.ppermute(block, axis, route)
-
-
-def collect_rows(own_piece, slices):
-    bit_count = slices.bit_length() - 1
-    for bit_pos in range(bit_count):
-        partner = partner_2(own_piece, "tok", bit_pos)
-        own_piece = jnp.concatenate([own_piece, partner], 0)
-    return own_piece
+def exchange_kernel(count, slices, groups, packed, out, own_sem, send, recv, pass_send, pass_recv):
+    me = lax.axis_index("tok")
+    barrier = pltpu.get_barrier_semaphore()
+    for d in range(1, count):
+        pl.semaphore_signal(
+            barrier,
+            inc=1,
+            device_id={"tok": lax.rem(me + d, count)},
+            device_id_type=pl.DeviceIdType.MESH,
+        )
+    pl.semaphore_wait(barrier, count - 1)
+    copies = []
+    for d in range(1, count):
+        target = lax.rem(me + d, count)
+        copies.append(
+            pltpu.make_async_remote_copy(
+                src_ref=packed.at[target],
+                dst_ref=out.at[0, d],
+                send_sem=send.at[d],
+                recv_sem=recv.at[d],
+                device_id={"tok": target},
+                device_id_type=pl.DeviceIdType.MESH,
+            )
+        )
+        copies[-1].start()
+    own = pltpu.make_async_copy(packed.at[me], out.at[0, 0], own_sem)
+    own.start()
+    own.wait()
+    base = me // slices * slices
+    size = count // groups
+    passed = []
+    for q in range(groups):
+        for d in range(max(1, q * size), (q + 1) * size):
+            copies[d - 1].wait_recv()
+        for p in range(1, slices):
+            partner = base + lax.rem(me - base + p, slices)
+            copy = pltpu.make_async_remote_copy(
+                src_ref=out.at[0, pl.ds(q * size, size)],
+                dst_ref=out.at[p, pl.ds(q * size, size)],
+                send_sem=pass_send.at[p - 1, q],
+                recv_sem=pass_recv.at[p - 1, q],
+                device_id={"tok": partner},
+                device_id_type=pl.DeviceIdType.MESH,
+            )
+            copy.start()
+            passed.append(copy)
+    for copy in copies:
+        copy.wait_send()
+    for copy in passed:
+        copy.wait()
+
+
+def exchange(packed, slices):
+    count, cap, features = packed.shape
+    groups = 4
+    return pl.pallas_call(
+        functools.partial(exchange_kernel, count, slices, groups),
+        out_shape=jax.ShapeDtypeStruct((slices, count, cap, features), packed.dtype),
+        in_specs=[pl.BlockSpec(memory_space=pltpu.HBM)],
+        out_specs=pl.BlockSpec(memory_space=pltpu.HBM),
+        scratch_shapes=[
+            pltpu.SemaphoreType.DMA,
+            pltpu.SemaphoreType.DMA((count,)),
+            pltpu.SemaphoreType.DMA((count,)),
+            pltpu.SemaphoreType.DMA((slices - 1, groups)),
+            pltpu.SemaphoreType.DMA((slices - 1, groups)),
+        ],
+        compiler_params=pltpu.CompilerParams(collective_id=0, has_side_effects=True),
+    )(packed)
 
 
 def slot_rows(target, slot_total, tokens):
@@ -241,6 +294,36 @@
     )(gathered)
 
 
+def whiten_kernel(columns, w_ref, u_ref, out_ref):
+    features = w_ref.shape[1]
+    for t in range(features // columns):
+
+        @pl.when(pl.program_id(1) == t)
+        def _():
+            out_ref[...] = lax.dot_general(
+                w_ref[:, t * columns :],
+                u_ref[:, t * columns :],
+                (((1,), (1,)), ((), ())),
+                preferred_element_type=jnp.float32,
+            ).astype(jnp.bfloat16)
+
+
+def whiten(weights, upper):
+    hidden, features = weights.shape
+    columns, block = 512, min(1024, hidden)
+    return pl.pallas_call(
+        functools.partial(whiten_kernel, columns),
+        out_shape=jax.ShapeDtypeStruct((hidden, features), jnp.bfloat16),
+        grid=(hidden // block, features // columns),
+        in_specs=[
+            pl.BlockSpec((block, features), lambda i, t: (i, 0)),
+            pl.BlockSpec((columns, features), lambda i, t: (t, 0)),
+        ],
+        out_specs=pl.BlockSpec((block, columns), lambda i, t: (i, t)),
+        compiler_params=pltpu.CompilerParams(vmem_limit_bytes=48 << 20),
+    )(weights, upper)
+
+
 def local(tokens, routes, weights):
     tok_devices = lax.axis_size("tok")
     slices = tok_devices // E
@@ -254,22 +337,10 @@
     slot_cap = most_rows // slices
     target = (picked * slices + ranked % slices) * slot_cap + ranked // slices
     packed = slot_rows(target, tok_devices * slot_cap, tokens)
-    received = lax.all_to_all(packed, "tok", split_axis=0, concat_axis=0, tiled=True)
-    gathered = collect_rows(received, slices)
+    gathered = exchange(packed.reshape(tok_devices, slot_cap, features), slices)
+    gathered = gathered.reshape(tok_devices * slices * slot_cap, features)
     upper = upper_factor(gathered)
-    band_width = features // NB
-    outputs = []
-    for section in range(NB):
-        lo = section * band_width
-        outputs.append(
-            lax.dot_general(
-                weights[:, lo:],
-                upper[lo : lo + band_width, lo:],
-                (((1,), (1,)), ((), ())),
-                preferred_element_type=jnp.float32,
-            ).astype(jnp.bfloat16)
-        )
-    return jnp.concatenate(outputs, 1)
+    return whiten(weights, upper)
 
 
 def solution(mesh):

time: 298 us -> 275 us (0.923); the launches traced: 295 us -> 275 us
  Pallas kernels: 185 us -> 262 us
  blocking collectives: 58.4 us -> 0 us
  matrix products: 25 us -> 0.66 us
  other arithmetic: 7.2 us -> 1.47 us
  local copies, waits for them, and re-layouts: 15.2 us -> 10.5 us
  waiting for transfers between devices: 3.86 us -> 0 us
    pallas_call x0 -> x2, Pallas kernels: none -> 77.4 us  [the longest x1 58.8 us: exchange(): pl.pallas_call(functools.partial(exchange_kernel, count, slices, groups),...]
    all_to_all x1 -> x0, blocking collectives: 58.4 us -> none  [local(): lax.all_to_all(packed, 'tok', split_axis=0, concat_axis=0, tiled=True)]
    dot_general x4 -> x0, matrix products: 23.1 us -> none  [local(): lax.dot_general(weights[:, lo:], upper[lo:lo + band_width, lo:], (((1,),...]
    reshape x0 -> x2, local copies, waits for them, and re-layouts: none -> 8.93 us  [the longest x1 6.88 us: local(): gathered = gathered.reshape(tok_devices * slices * slot_cap, features)]
    concatenate x1 -> x0, local copies, waits for them, and re-layouts: 8.61 us -> none  [local(): return jnp.concatenate(outputs, 1)]
    concatenate x2 -> x0, other arithmetic: 5.73 us -> none  [the longest x1 3.45 us: local(): return jnp.concatenate(outputs, 1)]
    all_to_all x2 -> x0, local copies, waits for them, and re-layouts: 5.03 us -> none  [local(): lax.all_to_all(packed, 'tok', split_axis=0, concat_axis=0, tiled=True)]
    ppermute x1 -> x0, waiting for transfers between devices: 3.86 us -> none  [partner_2(): return lax.ppermute(block, axis, route)]
  transfers between devices with their start and end apart: 1 -> 0, of which waited for: 1 -> 0; matrix products, arithmetic and copies ran while one was open for 0% -> 0% of each run, Pallas kernels for 0% -> 0%
where the time goes in v2:
time: 275 us
  Pallas kernels  262 us (95%)
  local copies, waits for them, and re-layouts  10.5 us (4%)
    pallas_call x1, Pallas kernels, upper_factor(): pl.pallas_call(factor_kernel, out_shape=jax.ShapeDtypeStruct((features, f...  185 us
    pallas_call x1, Pallas kernels, exchange(): pl.pallas_call(functools.partial(exchange_kernel, count, slices, groups),...  58.8 us
    pallas_call x1, Pallas kernels, whiten(): pl.pallas_call(functools.partial(whiten_kernel, columns), out_shape=jax.S...  18.5 us
    reshape x1, local copies, waits for them, and re-layouts, local(): gathered = gathered.reshape(tok_devices * slices * slot_cap, features)  6.88 us

profile of v2, /device:TPU:29, one launch (start us, length us, event | category | flops | bytes accessed | tf_op | source)
XLA Modules:
  0.0 274.8 jit_solution(8348613441876527811)
XLA Ops:
  0.0 0.0 copy-start
  0.0 0.9 copy.18
  0.9 0.1 eq.45
  1.0 0.1 eq.41
  1.2 0.6 reduce-window.6
  1.7 0.2 slice_reduce_fusion
  2.0 0.1 fusion.2
  2.1 0.1 reduce_sum.21
  2.2 0.1 copy.20
  2.3 0.7 fusion.5
  3.1 0.0 copy-done
  3.1 0.7 convolution_convert_fusion
  3.7 2.1 reshape.70.packed
  5.8 58.8 %shard_map.37 = bf16[2,16,20,3072]{3,2,1,0:T(8,128)(2,1)} custom-call(bf16[16,20,3072]{2,1,0:T(8,128)(2,1)} %reshape.70.packed), custom_call_target="tpu_custom_call" | custom-call | tf_op jit(solution)/shard_map/pallas_call | solution.py:73
  64.6 6.9 %reshape.71.x_ref = bf16[640,3072]{1,0:T(8,128)(2,1)} reshape(bf16[2,16,20,3072]{3,2,1,0:T(8,128)(2,1)} %shard_map.37) | data formatting | bytes 7864320 | tf_op jit(solution)/shard_map/reshape | solution.py:341
  71.5 184.7 %shard_map.38.u_ref = bf16[3072,3072]{1,0:T(8,128)(2,1)} custom-call(bf16[640,3072]{1,0:T(8,128)(2,1)} %reshape.71.x_ref), custom_call_target="tpu_custom_call" | custom-call | tf_op jit(solution)/shard_map/pallas_call | solution.py:277
  256.2 18.5 %shard_map.39 = bf16[1024,3072]{1,0:T(8,128)(2,1)} custom-call(bf16[1024,3072]{1,0:T(8,128)(2,1)} %w_ref.1, bf16[3072,3072]{1,0:T(8,128)(2,1)} %shard_map.38.u_ref), custom_call_target="tpu_custom_call" | custom-call | tf_op jit(solution)/shard_map/pallas_call | solution.py:314
  (4 shorter events, 0.1 us)
Async XLA Ops:
  0.0 3.1 %copy-start = (bf16[128,3072]{1,0:T(8,128)(2,1)S(1)}, bf16[128,3072]{1,0:T(8,128)(2,1)}, u32[]{:S(2)}) copy-start(bf16[128,3072]{1,0:T(8,128)(2,1)} %param.3) | copy-start | bytes 2359300
